TPU v7x, 32 devices: a whole 2x2x4 slice. The times are simulated.
32 devices in a mesh: seq: 8 (over z, x), head: 4 (over y, core).
Axes of the slice: x: 2, y: 2, z: 4, core: 2. Of those that a mesh axis runs over, the one named last changes fastest.
Arguments:
- h_in: float32 [2048, 1024], P('seq', 'head'), may hold values from -6 to 6
- norm_gain: float32 [2, 1024], P(None, 'head'), may hold values from 0.5 to 1.5
- w_z: bfloat16 [2, 1024, 2048], P(None, None, 'head'), may hold values from -0.1875 to 0.1875
- w_x: bfloat16 [2, 1024, 2048], P(None, None, 'head'), may hold values from -0.1875 to 0.1875
- w_bc: bfloat16 [2, 1024, 256], replicated, may hold values from -0.1875 to 0.1875
- w_dt: bfloat16 [2, 1024, 32], P(None, None, 'head'), may hold values from -0.1875 to 0.1875
- conv_x_w: float32 [2, 4, 2048], P(None, None, 'head'), may hold values from -3 to 3
- conv_x_b: float32 [2, 2048], P(None, 'head'), may hold values from -0.5 to 0.5
- conv_bc_w: float32 [2, 4, 256], replicated, may hold values from -3 to 3
- conv_bc_b: float32 [2, 256], replicated, may hold values from -0.5 to 0.5
- dt_bias: float32 [2, 32], P(None, 'head'), may hold values from -4 to -1
- a_log: float32 [2, 32], P(None, 'head'), may hold values from -10 to -1
- skip: float32 [2, 32], P(None, 'head'), may hold values from 0.5 to 1.5
- gate_gain: float32 [2, 2048], P(None, 'head'), may hold values from 0.5 to 1.5
- w_out: bfloat16 [2, 2048, 1024], P(None, 'head'), may hold values from -0.125 to 0.125
- d_out: float32 [2048, 1024], P('seq', 'head'), may hold values from -6 to 6
Outputs:
- h_out: float32 [2048, 1024], P('seq', 'head')
- d_h: float32 [2048, 1024], P('seq', 'head')
- d_norm_gain: float32 [2, 1024], P(None, 'head')
- d_w_z: float32 [2, 1024, 2048], P(None, 'seq', 'head')
- d_w_x: float32 [2, 1024, 2048], P(None, 'seq', 'head')
- d_w_bc: float32 [2, 1024, 256], replicated
- d_w_dt: float32 [2, 1024, 32], P(None, 'seq', 'head')
- d_conv_x_w: float32 [2, 4, 2048], P(None, None, 'head')
- d_conv_x_b: float32 [2, 2048], P(None, 'head')
- d_conv_bc_w: float32 [2, 4, 256], replicated
- d_conv_bc_b: float32 [2, 256], replicated
- d_dt_bias: float32 [2, 32], P(None, 'head')
- d_a_log: float32 [2, 32], P(None, 'head')
- d_skip: float32 [2, 32], P(None, 'head')
- d_gate_gain: float32 [2, 2048], P(None, 'head')
- d_w_out: float32 [2, 2048, 1024], P(None, 'head', 'seq')
All inputs are finite; a program needn't handle non-finite values.
Results may differ from a plain program's by a relative error of at most 0.014.
The roundings to bfloat16 on the way count: a program that leaves them out, or rounds other values in their place, can miss the bound.
Values may be sent and summed in bfloat16 or wider, within the bound.
A program may use at most 128 MiB of HBM per device.

v0:
```python
import jax
import jax.numpy as jnp
from jax import lax
from jax.sharding import PartitionSpec as P

D = 1024
HEAD_DIM = 64
STATE = 128
CONV = 4
SPAN = 256
LAYERS = 2
DI = 2048
epsilon = 1e-05
highest = lax.Precision.HIGHEST


def shifted(value, axis, steps):
    count = lax.axis_size(axis)
    first, last = (max(0, -steps), min(count, count - steps))
    return lax.ppermute(value, axis, [(source, source + steps) for source in range(first, last)])


def entering_2(value, axis, join, neutral, backward):
    count, mine = (lax.axis_size(axis), lax.axis_index(axis))
    pieces = jax.tree.map(lambda part: lax.all_gather(part, axis), value)
    if backward:
        pieces = jax.tree.map(lambda part: part[::-1], pieces)
        mine = count - 1 - mine
    total = jax.tree.map(
        lambda part, zero: jnp.full_like(part, 0) + jnp.asarray(zero, part.dtype), value, neutral
    )

    def lap(position, total):
        longer = join(total, jax.tree.map(lambda part: part[position], pieces))
        return jax.tree.map(lambda new, old: jnp.where(position < mine, new, old), longer, total)

    return lax.fori_loop(0, count - 1, lap, total)


def conv_inputs(extended, dt_raw, conv_weight, conv_bias, dt_bias, a_log):
    row_count = dt_raw.shape[0]
    mixed = jnp.zeros((row_count, extended.shape[1]), jnp.float32) + conv_bias[None, :]
    for offset in range(CONV):
        mixed = mixed + conv_weight[offset][None, :] * extended[offset : offset + row_count]
    active = jax.nn.silu(mixed)
    inner = extended.shape[1] - 2 * STATE
    head_count = dt_raw.shape[1]
    values = active[:, :inner].reshape(row_count, head_count, HEAD_DIM)
    b_proj = active[:, inner : inner + STATE]
    c_proj = active[:, inner + STATE :]
    steps_dt = jax.nn.softplus(dt_raw + dt_bias[None, :])
    log_decay = -steps_dt * jnp.exp(a_log)[None, :]
    return (values, b_proj, c_proj, steps_dt, log_decay)


def scan_from_zero(values, b_proj, c_proj, steps_dt, log_decay):
    row_count, head_count = steps_dt.shape
    blocks = row_count // SPAN
    causal = (jnp.arange(SPAN)[:, None] >= jnp.arange(SPAN)[None, :])[None]

    def one_block(carried, block_data):
        block_vals, b_blk, c_blk, dt_blk, la_blk = block_data
        cumulative = jnp.cumsum(la_blk, axis=0)
        cum_heads = cumulative.T
        spread = cum_heads[:, :, None] - cum_heads[:, None, :]
        weights = jnp.where(causal, jnp.exp(jnp.where(causal, spread, 0.0)), 0.0)
        scores = jnp.dot(c_blk, b_blk.T, precision=highest)
        scaled = block_vals * dt_blk[:, :, None]
        y_diag = jnp.einsum("htu,uhp->thp", weights * scores[None], scaled, precision=highest)
        y_off = (
            jnp.einsum("tn,hpn->thp", c_blk, carried, precision=highest)
            * jnp.exp(cumulative)[:, :, None]
        )
        ending = cumulative[-1]
        tail_decay = jnp.exp(ending[None, :] - cumulative)
        updated = carried * jnp.exp(ending)[:, None, None] + jnp.einsum(
            "uhp,un->hpn", scaled * tail_decay[:, :, None], b_blk, precision=highest
        )
        return (updated, y_diag + y_off)

    stacked = (
        values.reshape(blocks, SPAN, head_count, HEAD_DIM),
        b_proj.reshape(blocks, SPAN, STATE),
        c_proj.reshape(blocks, SPAN, STATE),
        steps_dt.reshape(blocks, SPAN, head_count),
        log_decay.reshape(blocks, SPAN, head_count),
    )
    initial = jnp.zeros((head_count, HEAD_DIM, STATE), jnp.float32)
    last_state, outputs = lax.scan(one_block, initial, stacked)
    return (outputs.reshape(row_count, head_count, HEAD_DIM), last_state)


def carry_term(c_proj, log_decay, entering):
    cumulative = jnp.cumsum(log_decay, axis=0)
    return (
        jnp.einsum("tn,hpn->thp", c_proj, entering, precision=highest)
        * jnp.exp(cumulative)[:, :, None]
    )


def link_states(earlier, later):
    return (earlier[0] * later[0], later[0][:, None, None] * earlier[1] + later[1])


def token_sums(partial_sums):
    return lax.psum(partial_sums, "head")


def contract_first(left, right):
    return lax.dot_general(
        left, right, (((0,), (0,)), ((), ())), preferred_element_type=jnp.float32
    )


def local(
    h_in,
    norm_gain,
    w_z,
    w_x,
    w_bc,
    w_dt,
    conv_x_w,
    conv_x_b,
    conv_bc_w,
    conv_bc_b,
    dt_bias,
    a_log,
    skip,
    gate_gain,
    w_out,
    d_out,
):
    row_count = h_in.shape[0]
    inner = w_x.shape[2]
    head_count = w_dt.shape[2]
    hidden = h_in
    kept = []
    for layer_idx in range(LAYERS):
        gain_one = norm_gain[layer_idx]
        full_hidden, full_gain = (
            lax.all_gather(hidden, "head", axis=1, tiled=True),
            lax.all_gather(gain_one, "head", axis=0, tiled=True),
        )
        factor = lax.rsqrt(jnp.mean(full_hidden * full_hidden, axis=1) + epsilon)
        normed = (full_hidden * factor[:, None] * full_gain[None, :]).astype(jnp.bfloat16)
        gate_in = jnp.dot(normed, w_z[layer_idx], preferred_element_type=jnp.float32)
        x_in = jnp.dot(normed, w_x[layer_idx], preferred_element_type=jnp.float32)
        bc_in = jnp.dot(normed, w_bc[layer_idx], preferred_element_type=jnp.float32)
        dt_raw = jnp.dot(normed, w_dt[layer_idx], preferred_element_type=jnp.float32)
        conv_in = jnp.concatenate([x_in, bc_in], axis=1)
        before = shifted(conv_in[row_count - (CONV - 1) :], "seq", 1)
        extended = jnp.concatenate([before, conv_in], axis=0)
        conv_weight = jnp.concatenate([conv_x_w[layer_idx], conv_bc_w[layer_idx]], axis=1)
        conv_bias = jnp.concatenate([conv_x_b[layer_idx], conv_bc_b[layer_idx]], axis=0)
        inputs, input_back = jax.vjp(
            conv_inputs,
            extended,
            dt_raw,
            conv_weight,
            conv_bias,
            dt_bias[layer_idx],
            a_log[layer_idx],
        )
        values, b_proj, c_proj, steps_dt, log_decay = inputs
        local_part, block_back = jax.vjp(
            scan_from_zero, values, b_proj, c_proj, steps_dt, log_decay
        )
        scanned, leaving = local_part
        decays = jnp.exp(jnp.sum(log_decay, axis=0))
        identity = (jnp.ones_like(decays), jnp.zeros_like(leaving))
        entering = entering_2((decays, leaving), "seq", link_states, identity, False)[1]
        carried_part, carry_back = jax.vjp(carry_term, c_proj, log_decay, entering)
        mixed = scanned + carried_part + skip[layer_idx][None, :, None] * values
        gate_act = jax.nn.silu(gate_in)
        gated = mixed.reshape(row_count, inner) * gate_act
        gate_factor = lax.rsqrt(token_sums(jnp.sum(gated * gated, axis=1)) / DI + epsilon)
        scaled = (gated * gate_factor[:, None] * gate_gain[layer_idx][None, :]).astype(jnp.bfloat16)
        out_weight = w_out[layer_idx]
        summed = lax.psum_scatter(
            contract_first(out_weight, scaled.T), "head", scatter_dimension=0, tiled=True
        )
        kept.append(
            (
                hidden,
                factor,
                normed,
                gate_in,
                gate_act,
                gated,
                gate_factor,
                scaled,
                mixed,
                values,
                decays,
                entering,
                input_back,
                block_back,
                carry_back,
            )
        )
        hidden = hidden + summed.T
    grad = d_out
    collected = [None] * LAYERS
    for layer_idx in reversed(range(LAYERS)):
        (
            layer_input,
            factor,
            normed,
            gate_in,
            gate_act,
            gated,
            gate_factor,
            scaled,
            mixed,
            values,
            decays,
            entering,
            input_back,
            block_back,
            carry_back,
        ) = kept[layer_idx]
        grad_b = grad.astype(jnp.bfloat16)
        out_weight = w_out[layer_idx]
        grad_cols = lax.all_gather(grad_b, "head", axis=1, tiled=True)
        d_part = lax.dot_general(
            grad_cols, out_weight, (((1,), (1,)), ((), ())), preferred_element_type=jnp.float32
        )
        d_cols = contract_first(scaled, grad_cols)
        normalized = gated * gate_factor[:, None]
        d_ggain = jnp.sum(d_part * normalized, axis=0)
        d_norm_in = d_part * gate_gain[layer_idx][None, :]
        along = token_sums(jnp.sum(d_norm_in * normalized, axis=1)) / DI
        d_gated = gate_factor[:, None] * (d_norm_in - normalized * along[:, None])
        sigma = jax.nn.sigmoid(gate_in)
        d_gate = d_gated * mixed.reshape(row_count, inner) * sigma * (1.0 + gate_in * (1.0 - sigma))
        d_mixed = (d_gated * gate_act).reshape(row_count, head_count, HEAD_DIM)
        d_skipped = jnp.sum(d_mixed * values, axis=(0, 2))
        d_c_carry, d_la_carry, d_entering = carry_back(d_mixed)
        back_identity = (jnp.ones_like(decays), jnp.zeros_like(d_entering))
        leaving_grad = entering_2((decays, d_entering), "seq", link_states, back_identity, True)[1]
        d_decays = jnp.sum(leaving_grad * entering, axis=(1, 2)) * decays
        d_values, d_b_proj, d_c_local, d_steps, d_la_local = block_back((d_mixed, leaving_grad))
        d_values = d_values + skip[layer_idx][None, :, None] * d_mixed
        d_inputs = (
            d_values,
            d_b_proj,
            d_c_carry + d_c_local,
            d_steps,
            d_la_carry + d_la_local + d_decays[None, :],
        )
        d_extended, d_dtraw, d_cweight, d_cbias, d_dtbias, d_alog = input_back(d_inputs)
        returned = shifted(d_extended[: CONV - 1], "seq", -1)
        d_conv = d_extended[CONV - 1 :] + jnp.pad(returned, ((row_count - (CONV - 1), 0), (0, 0)))
        d_gate_b = d_gate.astype(jnp.bfloat16)
        d_x_b = d_conv[:, :inner].astype(jnp.bfloat16)
        d_shared = d_conv[:, inner:]
        d_dt_b = d_dtraw.astype(jnp.bfloat16)
        d_wz = contract_first(normed, d_gate_b)
        d_wx = contract_first(normed, d_x_b)
        d_wdt = contract_first(normed, d_dt_b)
        d_wbc = lax.dot_general(
            normed.astype(jnp.float32), d_shared, (((0,), (0,)), ((), ())), precision=highest
        )
        wz_now = w_z[layer_idx]
        wx_now = w_x[layer_idx]
        wdt_now = w_dt[layer_idx]
        wbc_now = w_bc[layer_idx]

        def product(weight, grads):
            return lax.dot_general(
                weight, grads, (((1,), (1,)), ((), ())), preferred_element_type=jnp.float32
            )

        shared_rows = wbc_now.astype(jnp.float32)
        shared_term = lax.dot_general(
            shared_rows, d_shared, (((1,), (1,)), ((), ())), precision=highest
        )
        d_normed = lax.psum_scatter(
            product(wz_now, d_gate_b)
            + product(wx_now, d_x_b)
            + product(wdt_now, d_dt_b)
            + shared_term,
            "head",
            scatter_dimension=0,
            tiled=True,
        ).T
        centered = layer_input * factor[:, None]
        d_ngain = jnp.sum(d_normed * centered, axis=0)
        d_unit = d_normed * norm_gain[layer_idx][None, :]
        along_in = token_sums(jnp.sum(d_unit * centered, axis=1)) / D
        grad = grad + factor[:, None] * (d_unit - centered * along_in[:, None])
        collected[layer_idx] = (
            d_wz,
            d_wx,
            d_wdt,
            d_cols,
            d_ngain,
            d_cweight[:, :inner],
            d_cbias[:inner],
            d_ggain,
            d_dtbias,
            d_alog,
            d_skipped,
            d_wbc,
            d_cweight[:, inner:],
            d_cbias[inner:],
        )
    stacks = [
        jnp.stack([collected[layer_idx][member] for layer_idx in range(LAYERS)])
        for member in range(14)
    ]
    weight_sums = (
        lax.psum_scatter(
            stacks[0].astype(jnp.bfloat16), "seq", scatter_dimension=1, tiled=True
        ).astype(jnp.float32),
        lax.psum_scatter(
            stacks[1].astype(jnp.bfloat16), "seq", scatter_dimension=1, tiled=True
        ).astype(jnp.float32),
        lax.psum_scatter(
            stacks[2].astype(jnp.bfloat16), "seq", scatter_dimension=1, tiled=True
        ).astype(jnp.float32),
        lax.psum_scatter(
            stacks[3].astype(jnp.bfloat16), "seq", scatter_dimension=2, tiled=True
        ).astype(jnp.float32),
    )
    vector_sums = lax.psum(
        (stacks[4], stacks[5], stacks[6], stacks[7], stacks[8], stacks[9], stacks[10]), "seq"
    )
    shared_sums = lax.psum((stacks[11], stacks[12], stacks[13]), ("seq", "head"))
    return (
        hidden,
        grad,
        vector_sums[0],
        weight_sums[0],
        weight_sums[1],
        shared_sums[0],
        weight_sums[2],
        vector_sums[1],
        vector_sums[2],
        shared_sums[1],
        shared_sums[2],
        vector_sums[4],
        vector_sums[5],
        vector_sums[6],
        vector_sums[3],
        weight_sums[3],
    )


def solution(mesh):
    return jax.shard_map(
        local,
        mesh=mesh,
        in_specs=(
            P("seq", "head"),
            P(None, "head"),
            P(None, None, "head"),
            P(None, None, "head"),
            P(),
            P(None, None, "head"),
            P(None, None, "head"),
            P(None, "head"),
            P(),
            P(),
            P(None, "head"),
            P(None, "head"),
            P(None, "head"),
            P(None, "head"),
            P(None, "head", None),
            P("seq", "head"),
        ),
        out_specs=(
            P("seq", "head"),
            P("seq", "head"),
            P(None, "head"),
            P(None, "seq", "head"),
            P(None, "seq", "head"),
            P(),
            P(None, "seq", "head"),
            P(None, None, "head"),
            P(None, "head"),
            P(),
            P(),
            P(None, "head"),
            P(None, "head"),
            P(None, "head"),
            P(None, "head"),
            P(None, "head", "seq"),
        ),
        check_vma=False,
    )
```

profile of v0, /device:TPU:0, one launch (start us, length us, event | category | flops | bytes accessed | tf_op | source)
XLA Modules:
  0.0 995.1 jit_solution(10929443034664853142)
XLA Ops:
  8.7 6.0 all-gather
  22.1 6.9 all-gather.15.cloned.1.call-done
  45.5 21.2 %all-reduce.26 = f32[64]{0:T(128)S(1)} all-reduce(f32[64]{0:T(128)S(1)} %exponential_dynamic-update-slice_fusion.1), channel_id=3, replica_groups=mesh['seq'=8,'head'=4] {'seq'}, use_global_device_ids=true, to_apply=%add.26 | all-reduce | flops 64 | bytes 512
  68.5 23.3 %all-gather.19.cloned.1.call-done = f32[64,64,128]{2,1,0:T(8,128)} async-done(((f32[8,64,128]{2,1,0:T(8,128)}), f32[64,64,128]{2,1,0:T(8,128)}) %all-gather.19.cloned.1.call-update) | async-done | bytes 2097168 | tf_op jit(solution)/shard_map/all_gather | solution.py:25
  91.8 7.6 while.44
  109.1 5.8 psum.112
  117.8 23.7 %reduce-scatter.13.cloned.1.call-done = f32[256,256]{0,1:T(8,128)} async-done(((f32[1024,256]{0,1:T(8,128)}), f32[256,256]{0,1:T(8,128)}) %reduce-scatter.13.cloned.1.call-update) | async-done | bytes 262160 | tf_op jit(solution)/shard_map/reduce_scatter | solution.py:179
  149.6 10.6 %all-gather.17.cloned.1.call-done = f32[256,1024]{1,0:T(8,128)} async-done(((f32[256,256]{1,0:T(8,128)}), f32[256,1024]{1,0:T(8,128)}) %all-gather.17.cloned.1.call-update) | async-done | bytes 1048592 | tf_op jit(solution)/shard_map/all_gather | solution.py:141
  181.6 7.0 all_gather.64
  189.3 22.7 %all-reduce.27 = f32[64]{0:T(128)S(1)} all-reduce(f32[64]{0:T(128)S(1)} %exponential_dynamic-update-slice_fusion), channel_id=6, replica_groups=mesh['seq'=8,'head'=4] {'seq'}, use_global_device_ids=true, to_apply=%add.27 | all-reduce | flops 64 | bytes 512
  217.7 13.2 %all-gather.21.cloned.1.call-done = f32[64,64,128]{2,1,0:T(8,128)} async-done(((f32[8,64,128]{2,1,0:T(8,128)}), f32[64,64,128]{2,1,0:T(8,128)}) %all-gather.21.cloned.1.call-update) | async-done | bytes 2097168 | tf_op jit(solution)/shard_map/all_gather | solution.py:25
  230.9 15.9 %while.45 = (s32[]{:T(128)}, f32[8,64,128]{2,1,0:T(8,128)S(1)}, s32[]{:T(128)}, f32[8,8]{1,0:T(8,128)}, f32[8,8,64,128]{3,2,1,0:T(8,128)}, /*index=5*/s32[]{:T(128)}, s32[]{:T(128)}) while((s32[]{:T(128)}, f32[8,64,128]{2,1,0:T(8,128)S(1)}, s32[]{:T(128)}, f32[8,8]{1,0:T(8,128)}, f32[8,8,64,128]{3,2,1,0:T(8,128)}, ...), condition=%wide.region_14.16_spmd.clone, body=%wide.region_13.15_spmd.clone.sunk | while | flops 262148 | bytes 786633 | solution.py:37
  258.1 5.6 psum.113
  267.1 6.6 psum.114
  306.4 22.6 %all-gather.23.cloned.1.call-done = f32[64,64,128]{2,1,0:T(8,128)} async-done(((f32[8,64,128]{2,1,0:T(8,128)}), f32[64,64,128]{2,1,0:T(8,128)}) %all-gather.23.cloned.1.call-update) | async-done | bytes 2097168 | tf_op jit(solution)/shard_map/all_gather | solution.py:25
  332.1 15.8 %while.46 = (s32[]{:T(128)}, f32[8,64,128]{2,1,0:T(8,128)S(1)}, s32[]{:T(128)}, f32[8,8]{1,0:T(8,128)}, f32[8,8,64,128]{3,2,1,0:T(8,128)}, /*index=5*/s32[]{:T(128)}, s32[]{:T(128)}) while((s32[]{:T(128)}, f32[8,64,128]{2,1,0:T(8,128)S(1)}, s32[]{:T(128)}, f32[8,8]{1,0:T(8,128)}, f32[8,8,64,128]{3,2,1,0:T(8,128)}, ...), condition=%wide.region_22.24_spmd.clone, body=%wide.region_21.23_spmd.clone.sunk | while | flops 262148 | bytes 786633 | solution.py:37
  388.6 21.4 %reduce-scatter.17.cloned.1.call-done = f32[256,256]{0,1:T(8,128)} async-done(((f32[1024,256]{0,1:T(8,128)}), f32[256,256]{0,1:T(8,128)}) %reduce-scatter.17.cloned.1.call-update) | async-done | bytes 262160 | tf_op jit(solution)/shard_map/reduce_scatter | solution.py:278
  411.7 5.7 psum.115
  417.5 19.9 %reduce-scatter.15.cloned.1.call-done = f32[256,256]{0,1:T(8,128)} async-done(((f32[1024,256]{0,1:T(8,128)}), f32[256,256]{0,1:T(8,128)}) %reduce-scatter.15.cloned.1.call-update) | async-done | bytes 262160 | tf_op jit(solution)/shard_map/reduce_scatter | solution.py:179
  439.6 6.7 all_gather.67
  449.0 6.7 psum.116
  475.4 35.6 %all-gather.25.cloned.1.call-done = f32[64,64,128]{2,1,0:T(8,128)} async-done(((f32[8,64,128]{2,1,0:T(8,128)}), f32[64,64,128]{2,1,0:T(8,128)}) %all-gather.25.cloned.1.call-update) | async-done | bytes 2097168 | tf_op jit(solution)/shard_map/all_gather | solution.py:25
  514.2 12.3 %while.47 = (s32[]{:T(128)}, f32[8,64,128]{2,1,0:T(8,128)S(1)}, s32[]{:T(128)}, f32[8,8]{1,0:T(8,128)}, f32[8,8,64,128]{3,2,1,0:T(8,128)}, /*index=5*/s32[]{:T(128)}, s32[]{:T(128)}) while((s32[]{:T(128)}, f32[8,64,128]{2,1,0:T(8,128)S(1)}, s32[]{:T(128)}, f32[8,8]{1,0:T(8,128)}, f32[8,8,64,128]{3,2,1,0:T(8,128)}, ...), condition=%wide.region_43.45_spmd.clone, body=%wide.region_42.44_spmd.clone.sunk | while | flops 262148 | bytes 786633 | solution.py:37
  546.2 6.2 copy.152
  597.7 41.8 %all-reduce.28 = (f32[2,4,256]{2,1,0:T(4,128)}, f32[2,256]{1,0:T(2,128)}) all-reduce(f32[2,4,256]{2,1,0:T(4,128)S(1)} %pad_maximum_fusion.8, f32[2,256]{1,0:T(2,128)S(1)} %pad_maximum_fusion.16), channel_id=1, replica_groups=mesh['seq'=8,'head'=4] {'seq','head'}, use_global_device_ids=true, to_apply=%region_79.81 | all-reduce | flops 2560 | bytes 20480 | tf_op jit(solution)/shard_map/psum | solution.py:329
  643.6 31.7 %reduce-scatter.27.cloned.1.call-done = bf16[128,1024]{1,0:T(8,128)(2,1)} async-done(((bf16[1024,1024]{1,0:T(8,128)(2,1)}), bf16[128,1024]{1,0:T(8,128)(2,1)}) %reduce-scatter.27.cloned.1.call-update) | async-done | bytes 262160
  677.5 69.4 %reduce-scatter.21.cloned.1.call-done = bf16[2,128,512]{2,1,0:T(8,128)(2,1)} async-done(((bf16[2,1024,512]{2,1,0:T(8,128)(2,1)}), bf16[2,128,512]{2,1,0:T(8,128)(2,1)}) %reduce-scatter.21.cloned.1.call-update) | async-done | bytes 262160 | tf_op jit(solution)/shard_map/reduce_scatter | solution.py:313
  748.7 24.5 %reduce-scatter.19.cloned.1.call-done = f32[256,256]{0,1:T(8,128)} async-done(((f32[1024,256]{0,1:T(8,128)}), f32[256,256]{0,1:T(8,128)}) %reduce-scatter.19.cloned.1.call-update) | async-done | bytes 262160 | tf_op jit(solution)/shard_map/reduce_scatter | solution.py:278
  774.4 5.8 psum.117
  780.1 38.2 %all-reduce.29 = (f32[2,256]{1,0:T(2,128)}, f32[2,4,512]{2,1,0:T(4,128)}, f32[2,512]{1,0:T(2,128)}, f32[2,8]{1,0:T(2,128)}, f32[2,8]{1,0:T(2,128)}, /*index=5*/f32[2,8]{1,0:T(2,128)}, f32[2,512]{1,0:T(2,128)}) all-reduce(f32[2,256]{1,0:T(2,128)S(1)} %pad_maximum_fusion.15, ...), channel_id=1, replica_groups=mesh['seq'=8,'head'=4] {'seq'}, use_global_device_ids=true, to_apply=%region_62.64 | all-reduce | flops 6704 | bytes 53632 | tf_op jit(solution)/shard_map/psum | solution.py:326
  820.2 25.9 %reduce-scatter.23.cloned.1.call-done = bf16[2,128,512]{2,1,0:T(8,128)(2,1)} async-done(((bf16[2,1024,512]{2,1,0:T(8,128)(2,1)}), bf16[2,128,512]{2,1,0:T(8,128)(2,1)}) %reduce-scatter.23.cloned.1.call-update) | async-done | bytes 262160 | tf_op jit(solution)/shard_map/reduce_scatter | solution.py:316
  847.9 137.2 %all-reduce.32.cloned.1.call-done = f32[2,1024,256]{2,1,0:T(8,128)} async-done(((f32[2,1024,256]{2,1,0:T(8,128)}), f32[2,1024,256]{2,1,0:T(8,128)}) %all-reduce.32.cloned.1.call-update) | async-done | bytes 2097168 | tf_op jit(solution)/shard_map/psum | solution.py:329
  (630 shorter events, 325.7 us)
Async XLA Ops:
  7.2 21.8 %all-gather.15.cloned.1.call-start = ((), (), s32[]{:S(2)}) async-start(), calls=%async_computation.8 | async-start | bytes 1310720 | tf_op jit(solution)/shard_map/all_gather | solution.py:141
  7.9 83.9 %all-gather.19.cloned.1.call-start = ((), (), s32[]{:S(2)}) async-start(), calls=%async_computation.17 | async-start | bytes 2359296 | tf_op jit(solution)/shard_map/all_gather | solution.py:25
  8.7 134.5 %copy-start.103 = (f32[1,256]{1,0:T(1,128)}, f32[1,256]{1,0:T(1,128)S(1)}, u32[]{:S(2)}) copy-start(f32[1,256]{1,0:T(1,128)S(1)} %get-tuple-element.1312) | copy-start | bytes 3076
  32.9 6.0 collective-permute-start
  40.3 59.1 %copy-start = (f32[256,768]{1,0:T(8,128)}, f32[256,768]{1,0:T(8,128)S(1)}, u32[]{:S(2)}) copy-start(f32[256,768]{1,0:T(8,128)S(1)} %get-tuple-element.1275) | copy-start | bytes 2359300
  40.7 59.4 %copy-start.17 = (f32[256,512]{0,1:T(8,128)}, f32[256,512]{0,1:T(8,128)S(1)}, u32[]{:S(2)}) copy-start(f32[256,512]{0,1:T(8,128)S(1)} %copy.129) | copy-start | bytes 1572868
  42.3 99.1 %reduce-scatter.13.cloned.1.call-start = ((), (), s32[]{:S(2)}) async-start(), calls=%async_computation.9 | async-start | bytes 1310720 | tf_op jit(solution)/shard_map/reduce_scatter | solution.py:179
  44.8 55.2 %copy-start.134 = (f32[8]{0:T(128)}, f32[8]{0:T(128)S(1)}, u32[]{:S(2)}) copy-start(f32[8]{0:T(128)S(1)} %get-tuple-element.1317) | copy-start | bytes 100
  45.4 69.5 %copy-start.88 = (f32[1,512]{1,0:T(1,128)}, f32[1,512]{1,0:T(1,128)S(1)}, u32[]{:S(2)}) copy-start(f32[1,512]{1,0:T(1,128)S(1)} %get-tuple-element.1307) | copy-start | bytes 6148
  117.7 42.5 %all-gather.17.cloned.1.call-start = ((), (), s32[]{:S(2)}) async-start(), calls=%async_computation.10 | async-start | bytes 1310720 | tf_op jit(solution)/shard_map/all_gather | solution.py:141
  143.2 87.7 %all-gather.21.cloned.1.call-start = ((), (), s32[]{:S(2)}) async-start(), calls=%async_computation.18 | async-start | bytes 2359296 | tf_op jit(solution)/shard_map/all_gather | solution.py:25
  167.1 4.8 collective-permute-start.1
  180.5 148.4 %all-gather.23.cloned.1.call-start = ((), (), s32[]{:S(2)}) async-start(), calls=%async_computation.19 | async-start | bytes 2359296 | tf_op jit(solution)/shard_map/all_gather | solution.py:25
  281.6 128.5 %reduce-scatter.17.cloned.1.call-start = ((), (), s32[]{:S(2)}) async-start(), calls=%async_computation.12 | async-start | bytes 1310720 | tf_op jit(solution)/shard_map/reduce_scatter | solution.py:278
  376.8 5.6 collective-permute-start.2
  385.7 51.7 %reduce-scatter.15.cloned.1.call-start = ((), (), s32[]{:S(2)}) async-start(), calls=%async_computation.11 | async-start | bytes 1310720 | tf_op jit(solution)/shard_map/reduce_scatter | solution.py:179
  388.5 58.5 %copy-start.23 = (f32[256,512]{1,0:T(8,128)S(1)}, f32[256,512]{1,0:T(8,128)}, u32[]{:S(2)}) copy-start(f32[256,512]{1,0:T(8,128)} %copy-done.22) | copy-start | bytes 1572868
  388.5 58.5 %copy-start.89 = (f32[1,512]{1,0:T(1,128)S(1)}, f32[1,512]{1,0:T(1,128)}, u32[]{:S(2)}) copy-start(f32[1,512]{1,0:T(1,128)} %copy-done.88) | copy-start | bytes 6148
  388.5 58.5 %copy-start.94 = (f32[256]{0:T(256)S(1)}, f32[256]{0:T(256)}, u32[]{:S(2)}) copy-start(f32[256]{0:T(256)} %copy-done.93) | copy-start | bytes 3076
  388.6 122.4 %all-gather.25.cloned.1.call-start = ((), (), s32[]{:S(2)}) async-start(), calls=%async_computation.20 | async-start | bytes 2359296 | tf_op jit(solution)/shard_map/all_gather | solution.py:25
  461.4 180.5 %reduce-scatter.25.cloned.1.call-start = ((), (), s32[]{:S(2)}) async-start(), calls=%async_computation.21 | async-start | bytes 294912
  543.1 132.2 %reduce-scatter.27.cloned.1.call-start = ((), (), s32[]{:S(2)}) async-start(), calls=%async_computation.22 | async-start | bytes 2359296
  555.9 191.0 %reduce-scatter.21.cloned.1.call-start = ((), (), s32[]{:S(2)}) async-start(), calls=%async_computation.14 | async-start | bytes 2359296 | tf_op jit(solution)/shard_map/reduce_scatter | solution.py:313
  560.2 213.0 %reduce-scatter.19.cloned.1.call-start = ((), (), s32[]{:S(2)}) async-start(), calls=%async_computation.13 | async-start | bytes 1310720 | tf_op jit(solution)/shard_map/reduce_scatter | solution.py:278
  583.2 5.9 collective-permute-start.3
  592.1 254.0 %reduce-scatter.23.cloned.1.call-start = ((), (), s32[]{:S(2)}) async-start(), calls=%async_computation.15 | async-start | bytes 2359296 | tf_op jit(solution)/shard_map/reduce_scatter | solution.py:316
  594.8 390.2 %all-reduce.32.cloned.1.call-start = ((), (), s32[]{:S(2)}) async-start(), calls=%async_computation.16 | async-start | bytes 4194304 | tf_op jit(solution)/shard_map/psum | solution.py:329
  641.8 131.4 %copy-start.29 = (f32[256,256]{1,0:T(8,128)S(1)}, f32[256,256]{1,0:T(8,128)}, u32[]{:S(2)}) copy-start(f32[256,256]{1,0:T(8,128)} %param.25) | copy-start | bytes 786436
  641.9 131.4 %copy-start.102 = (f32[1,256]{1,0:T(1,128)S(1)}, f32[1,256]{1,0:T(1,128)}, u32[]{:S(2)}) copy-start(f32[1,256]{1,0:T(1,128)} %copy-done.101) | copy-start | bytes 3076
  641.9 131.4 %copy-start.109 = (f32[256]{0:T(256)S(1)}, f32[256]{0:T(256)}, u32[]{:S(2)}) copy-start(f32[256]{0:T(256)} %copy-done.108) | copy-start | bytes 3076
  641.9 138.2 %copy-start.123 = (f32[256]{0:T(256)S(1)}, f32[256]{0:T(256)}, u32[]{:S(2)}) copy-start(f32[256]{0:T(256)} %get-tuple-element.1182) | copy-start | bytes 3076
  641.9 176.5 %copy-start.55 = (f32[256,256]{1,0:T(8,128)S(1)}, f32[256,256]{1,0:T(8,128)}, u32[]{:S(2)}) copy-start(f32[256,256]{1,0:T(8,128)} %get-tuple-element.1264) | copy-start | bytes 786436
  (130 other events, 1273.8 us)
Sparse Core Ops, SparseCore 0:
  9.5 19.4 all-gather.14
  42.4 49.3 all-gather.18
  117.8 23.5 reduce-scatter.12
  143.4 16.6 all-gather.16
  180.7 50.1 all-gather.20
  281.7 47.2 all-gather.22
  385.8 24.1 reduce-scatter.16
  412.6 24.7 reduce-scatter.14
  461.5 49.4 all-gather.24
  543.2 60.5 reduce-scatter.24
  607.4 67.9 reduce-scatter.26
  679.3 67.6 reduce-scatter.20
  749.5 23.7 reduce-scatter.18
  776.6 69.4 reduce-scatter.22
  851.3 133.7 all-reduce.31
where the time goes:
time: 1010 us; the launch traced here: 995 us
  waiting for transfers between devices  475 us (47%)
  blocking collectives  185 us (18%)
  other arithmetic  110 us (11%)
  matrix products  100 us (10%)
  local copies, waits for them, and re-layouts  96.9 us (10%)
  between operations  17.1 us (2%)
  starting transfers between devices  10.5 us (1%)
    psum x1, waiting for transfers between devices, local(): lax.psum((stacks[11], stacks[12], stacks[13]), ('seq', 'head'))  137 us
    all_gather x4, waiting for transfers between devices, entering_2(): pieces = jax.tree.map(lambda part: lax.all_gather(part, axis), value)  94.6 us
    reduce_scatter x1, waiting for transfers between devices, local(): lax.psum_scatter(stacks[0].astype(jnp.bfloat16), 'seq', scatter_dimension...  69.4 us
    reduce_scatter x2, waiting for transfers between devices, local(): lax.psum_scatter(product(wz_now, d_gate_b) + product(wx_now, d_x_b) + pro...  45.9 us
    unnamed x2, blocking collectives  43.9 us
    reduce_scatter x2, waiting for transfers between devices, local(): lax.psum_scatter(contract_first(out_weight, scaled.T), 'head', scatter_di...  43.6 us
    psum x1, blocking collectives, local(): lax.psum((stacks[11], stacks[12], stacks[13]), ('seq', 'head'))  41.8 us
    psum x1, blocking collectives, local(): lax.psum((stacks[4], stacks[5], stacks[6], stacks[7], stacks[8], stacks[9...  38.2 us
  transfers between devices with their start and end apart: 19, of which 17 were waited for; matrix products, arithmetic and copies ran while one was open for 13% of the time, Pallas kernels for 0%

commit v1 on v0

--- a/solution.py
+++ b/solution.py
@@ -326,7 +326,7 @@
     vector_sums = lax.psum(
         (stacks[4], stacks[5], stacks[6], stacks[7], stacks[8], stacks[9], stacks[10]), "seq"
     )
-    shared_sums = lax.psum((stacks[11], stacks[12], stacks[13]), ("seq", "head"))
+    shared_sums = lax.psum(lax.psum((stacks[11], stacks[12], stacks[13]), "head"), "seq")
     return (
         hidden,
         grad,

time: 1010 us -> 1050 us (1.040)
  waiting for transfers between devices: 475 us -> 550 us
  blocking collectives: 185 us -> 148 us
    unnamed x17 -> x18, waiting for transfers between devices: 32.7 us -> 136 us
    psum x1 -> x0, blocking collectives: 41.8 us -> none  [local(): lax.psum((stacks[11], stacks[12], stacks[13]), ('seq', 'head'))]
    psum x1 -> x2, waiting for transfers between devices: 137 us -> 124 us  [the longest x1 103 us: local(): lax.psum(lax.psum((stacks[11], stacks[12], stacks[13]), 'head'), 'seq')]
    unnamed x300 -> x320, local copies, waits for them, and re-layouts: 26.8 us -> 25.3 us
  transfers between devices with their start and end apart: 19 -> 20, of which waited for: 17 -> 19; matrix products, arithmetic and copies ran while one was open for 13% -> 11% of each run, Pallas kernels for 0% -> 0%
where the time goes in v1:
time: 1050 us; the launch traced here: 1040 us
  waiting for transfers between devices  550 us (52%)
  blocking collectives  148 us (14%)
  other arithmetic  120 us (11%)
  matrix products  101 us (10%)
  local copies, waits for them, and re-layouts  95.4 us (9%)
  between operations  17.1 us (2%)
    unnamed x18, waiting for transfers between devices  136 us
    psum x1, waiting for transfers between devices, local(): lax.psum(lax.psum((stacks[11], stacks[12], stacks[13]), 'head'), 'seq')  103 us
    all_gather x4, waiting for transfers between devices, entering_2(): pieces = jax.tree.map(lambda part: lax.all_gather(part, axis), value)  85.7 us
    reduce_scatter x1, waiting for transfers between devices, local(): lax.psum_scatter(stacks[0].astype(jnp.bfloat16), 'seq', scatter_dimension...  69.4 us
    reduce_scatter x2, waiting for transfers between devices, local(): lax.psum_scatter(product(wz_now, d_gate_b) + product(wx_now, d_x_b) + pro...  45.9 us
    unnamed x2, blocking collectives  43.7 us
    reduce_scatter x2, waiting for transfers between devices, local(): lax.psum_scatter(contract_first(out_weight, scaled.T), 'head', scatter_di...  43.6 us
    psum x6, blocking collectives, token_sums(): return lax.psum(partial_sums, 'head')  40.5 us
  transfers between devices with their start and end apart: 20, of which 19 were waited for; matrix products, arithmetic and copies ran while one was open for 11% of the time, Pallas kernels for 0%

profile of v1, /device:TPU:0, one launch (start us, length us, event | category | flops | bytes accessed | tf_op | source)
XLA Modules:
  0.0 1041.9 jit_solution(17778061843985212667)
XLA Ops:
  8.7 6.0 all-gather
  22.1 6.9 all-gather.15.cloned.1.call-done
  45.6 21.2 %all-reduce.26 = f32[64]{0:T(128)S(1)} all-reduce(f32[64]{0:T(128)S(1)} %exponential_dynamic-update-slice_fusion.1), channel_id=3, replica_groups=mesh['seq'=8,'head'=4] {'seq'}, use_global_device_ids=true, to_apply=%add.26 | all-reduce | flops 64 | bytes 512
  68.6 23.0 %all-gather.19.cloned.1.call-done = f32[64,64,128]{2,1,0:T(8,128)} async-done(((f32[8,64,128]{2,1,0:T(8,128)}), f32[64,64,128]{2,1,0:T(8,128)}) %all-gather.19.cloned.1.call-update) | async-done | bytes 2097168 | tf_op jit(solution)/shard_map/all_gather | solution.py:25
  91.6 7.6 while.44
  108.9 5.8 psum.133
  117.6 23.7 %reduce-scatter.13.cloned.1.call-done = f32[256,256]{0,1:T(8,128)} async-done(((f32[1024,256]{0,1:T(8,128)}), f32[256,256]{0,1:T(8,128)}) %reduce-scatter.13.cloned.1.call-update) | async-done | bytes 262160 | tf_op jit(solution)/shard_map/reduce_scatter | solution.py:179
  149.4 10.6 %all-gather.17.cloned.1.call-done = f32[256,1024]{1,0:T(8,128)} async-done(((f32[256,256]{1,0:T(8,128)}), f32[256,1024]{1,0:T(8,128)}) %all-gather.17.cloned.1.call-update) | async-done | bytes 1048592 | tf_op jit(solution)/shard_map/all_gather | solution.py:141
  181.4 7.0 all_gather.64
  189.1 22.5 %all-reduce.27 = f32[64]{0:T(128)S(1)} all-reduce(f32[64]{0:T(128)S(1)} %exponential_dynamic-update-slice_fusion), channel_id=6, replica_groups=mesh['seq'=8,'head'=4] {'seq'}, use_global_device_ids=true, to_apply=%add.27 | all-reduce | flops 64 | bytes 512
  217.4 13.3 %all-gather.21.cloned.1.call-done = f32[64,64,128]{2,1,0:T(8,128)} async-done(((f32[8,64,128]{2,1,0:T(8,128)}), f32[64,64,128]{2,1,0:T(8,128)}) %all-gather.21.cloned.1.call-update) | async-done | bytes 2097168 | tf_op jit(solution)/shard_map/all_gather | solution.py:25
  230.7 15.9 %while.45 = (s32[]{:T(128)}, f32[8,64,128]{2,1,0:T(8,128)S(1)}, s32[]{:T(128)}, f32[8,8]{1,0:T(8,128)}, f32[8,8,64,128]{3,2,1,0:T(8,128)}, /*index=5*/s32[]{:T(128)}, s32[]{:T(128)}) while((s32[]{:T(128)}, f32[8,64,128]{2,1,0:T(8,128)S(1)}, s32[]{:T(128)}, f32[8,8]{1,0:T(8,128)}, f32[8,8,64,128]{3,2,1,0:T(8,128)}, ...), condition=%wide.region_14.16_spmd.clone, body=%wide.region_13.15_spmd.clone.sunk | while | flops 262148 | bytes 786633 | solution.py:37
  266.9 6.6 psum.135
  306.2 22.5 %all-gather.23.cloned.1.call-done = f32[64,64,128]{2,1,0:T(8,128)} async-done(((f32[8,64,128]{2,1,0:T(8,128)}), f32[64,64,128]{2,1,0:T(8,128)}) %all-gather.23.cloned.1.call-update) | async-done | bytes 2097168 | tf_op jit(solution)/shard_map/all_gather | solution.py:25
  331.9 15.8 %while.46 = (s32[]{:T(128)}, f32[8,64,128]{2,1,0:T(8,128)S(1)}, s32[]{:T(128)}, f32[8,8]{1,0:T(8,128)}, f32[8,8,64,128]{3,2,1,0:T(8,128)}, /*index=5*/s32[]{:T(128)}, s32[]{:T(128)}) while((s32[]{:T(128)}, f32[8,64,128]{2,1,0:T(8,128)S(1)}, s32[]{:T(128)}, f32[8,8]{1,0:T(8,128)}, f32[8,8,64,128]{3,2,1,0:T(8,128)}, ...), condition=%wide.region_22.24_spmd.clone, body=%wide.region_21.23_spmd.clone.sunk | while | flops 262148 | bytes 786633 | solution.py:37
  358.7 13.6 %reduce-window.90 = f32[8,2,128]{2,0,1:T(8,128)S(1)} reduce-window(f32[8,2,128]{2,0,1:T(8,128)S(1)} %fusion.248, f32[]{:T(128)} %constant.312.clone.1), window={size=1x1x128 pad=0_0x0_0x0_127}, to_apply=%region_33.35 | reduce-window | flops 260096 | bytes 16388 | tf_op jit(solution)/shard_map/reduce-window.24
  399.3 21.4 %reduce-scatter.17.cloned.1.call-done = f32[256,256]{0,1:T(8,128)} async-done(((f32[1024,256]{0,1:T(8,128)}), f32[256,256]{0,1:T(8,128)}) %reduce-scatter.17.cloned.1.call-update) | async-done | bytes 262160 | tf_op jit(solution)/shard_map/reduce_scatter | solution.py:278
  428.1 19.9 %reduce-scatter.15.cloned.1.call-done = f32[256,256]{0,1:T(8,128)} async-done(((f32[1024,256]{0,1:T(8,128)}), f32[256,256]{0,1:T(8,128)}) %reduce-scatter.15.cloned.1.call-update) | async-done | bytes 262160 | tf_op jit(solution)/shard_map/reduce_scatter | solution.py:179
  450.2 6.7 all_gather.67
  459.6 6.7 psum.137
  494.8 26.9 %all-gather.25.cloned.1.call-done = f32[64,64,128]{2,1,0:T(8,128)} async-done(((f32[8,64,128]{2,1,0:T(8,128)}), f32[64,64,128]{2,1,0:T(8,128)}) %all-gather.25.cloned.1.call-update) | async-done | bytes 2097168 | tf_op jit(solution)/shard_map/all_gather | solution.py:25
  524.8 12.5 %while.47 = (s32[]{:T(128)}, f32[8,64,128]{2,1,0:T(8,128)S(1)}, s32[]{:T(128)}, f32[8,8]{1,0:T(8,128)}, f32[8,8,64,128]{3,2,1,0:T(8,128)}, /*index=5*/s32[]{:T(128)}, s32[]{:T(128)}) while((s32[]{:T(128)}, f32[8,64,128]{2,1,0:T(8,128)S(1)}, s32[]{:T(128)}, f32[8,8]{1,0:T(8,128)}, f32[8,8,64,128]{3,2,1,0:T(8,128)}, ...), condition=%wide.region_43.45_spmd.clone, body=%wide.region_42.44_spmd.clone.sunk | while | flops 262148 | bytes 786633 | solution.py:37
  577.1 6.2 copy.152
  598.9 20.8 %all-reduce.33.cloned.1.call-done = f32[2,1024,256]{2,1,0:T(8,128)} async-done(((f32[2,1024,256]{2,1,0:T(8,128)}), f32[2,1024,256]{2,1,0:T(8,128)}) %all-reduce.33.cloned.1.call-update) | async-done | bytes 2097168 | tf_op jit(solution)/shard_map/psum | solution.py:329
  620.4 65.5 %reduce-scatter.25.cloned.1.call-done = bf16[128,16]{1,0:T(8,128)(2,1)} async-done(((bf16[1024,16]{1,0:T(8,128)(2,1)}), bf16[128,16]{1,0:T(8,128)(2,1)}) %reduce-scatter.25.cloned.1.call-update) | async-done | bytes 4112
  687.4 69.3 %reduce-scatter.27.cloned.1.call-done = bf16[128,1024]{1,0:T(8,128)(2,1)} async-done(((bf16[1024,1024]{1,0:T(8,128)(2,1)}), bf16[128,1024]{1,0:T(8,128)(2,1)}) %reduce-scatter.27.cloned.1.call-update) | async-done | bytes 262160
  758.9 69.4 %reduce-scatter.21.cloned.1.call-done = bf16[2,128,512]{2,1,0:T(8,128)(2,1)} async-done(((bf16[2,1024,512]{2,1,0:T(8,128)(2,1)}), bf16[2,128,512]{2,1,0:T(8,128)(2,1)}) %reduce-scatter.21.cloned.1.call-update) | async-done | bytes 262160 | tf_op jit(solution)/shard_map/reduce_scatter | solution.py:313
  830.1 24.5 %reduce-scatter.19.cloned.1.call-done = f32[256,256]{0,1:T(8,128)} async-done(((f32[1024,256]{0,1:T(8,128)}), f32[256,256]{0,1:T(8,128)}) %reduce-scatter.19.cloned.1.call-update) | async-done | bytes 262160 | tf_op jit(solution)/shard_map/reduce_scatter | solution.py:278
  855.7 10.1 all-reduce.29
  865.8 38.5 %all-reduce.28 = (f32[2,256]{1,0:T(2,128)}, f32[2,4,512]{2,1,0:T(4,128)}, f32[2,512]{1,0:T(2,128)}, f32[2,4,256]{2,1,0:T(4,128)}, f32[2,256]{1,0:T(2,128)}, /*in...) all-reduce(f32[2,256]{1,0:T(2,128)S(1)} %pad_maximum_fusion.15, ...), channel_id=1, replica_groups=mesh['seq'=8,'head'=4] {'seq'}, use_global_device_ids=true, to_apply=%region_62.64 | all-reduce | flops 9264 | bytes 74112 | tf_op jit(solution)/shard_map/psum | solution.py:326
  906.1 20.9 %reduce-scatter.23.cloned.1.call-done = bf16[2,128,512]{2,1,0:T(8,128)(2,1)} async-done(((bf16[2,1024,512]{2,1,0:T(8,128)(2,1)}), bf16[2,128,512]{2,1,0:T(8,128)(2,1)}) %reduce-scatter.23.cloned.1.call-update) | async-done | bytes 262160 | tf_op jit(solution)/shard_map/reduce_scatter | solution.py:316
  928.9 103.0 %all-reduce.35.cloned.1.call-done = f32[2,1024,256]{2,1,0:T(8,128)} async-done(((f32[2,1024,256]{2,1,0:T(8,128)}), f32[2,1024,256]{2,1,0:T(8,128)}) %all-reduce.35.cloned.1.call-update) | async-done | bytes 2097168 | tf_op jit(solution)/shard_map/psum | solution.py:329
  (652 shorter events, 331.6 us)
Async XLA Ops:
  7.2 21.8 %all-gather.15.cloned.1.call-start = ((), (), s32[]{:S(2)}) async-start(), calls=%async_computation.8 | async-start | bytes 1310720 | tf_op jit(solution)/shard_map/all_gather | solution.py:141
  7.9 83.7 %all-gather.19.cloned.1.call-start = ((), (), s32[]{:S(2)}) async-start(), calls=%async_computation.18 | async-start | bytes 2359296 | tf_op jit(solution)/shard_map/all_gather | solution.py:25
  8.7 134.3 %copy-start.105 = (f32[1,256]{1,0:T(1,128)}, f32[1,256]{1,0:T(1,128)S(1)}, u32[]{:S(2)}) copy-start(f32[1,256]{1,0:T(1,128)S(1)} %get-tuple-element.1315) | copy-start | bytes 3076
  32.9 6.1 collective-permute-start
  40.4 58.9 %copy-start = (f32[256,768]{1,0:T(8,128)}, f32[256,768]{1,0:T(8,128)S(1)}, u32[]{:S(2)}) copy-start(f32[256,768]{1,0:T(8,128)S(1)} %get-tuple-element.1278) | copy-start | bytes 2359300
  40.7 59.1 %copy-start.19 = (f32[256,512]{0,1:T(8,128)}, f32[256,512]{0,1:T(8,128)S(1)}, u32[]{:S(2)}) copy-start(f32[256,512]{0,1:T(8,128)S(1)} %copy.129) | copy-start | bytes 1572868
  42.4 98.9 %reduce-scatter.13.cloned.1.call-start = ((), (), s32[]{:S(2)}) async-start(), calls=%async_computation.9 | async-start | bytes 1310720 | tf_op jit(solution)/shard_map/reduce_scatter | solution.py:179
  45.5 69.3 %copy-start.90 = (f32[1,512]{1,0:T(1,128)}, f32[1,512]{1,0:T(1,128)S(1)}, u32[]{:S(2)}) copy-start(f32[1,512]{1,0:T(1,128)S(1)} %get-tuple-element.1310) | copy-start | bytes 6148
  117.5 42.5 %all-gather.17.cloned.1.call-start = ((), (), s32[]{:S(2)}) async-start(), calls=%async_computation.10 | async-start | bytes 1310720 | tf_op jit(solution)/shard_map/all_gather | solution.py:141
  143.0 87.7 %all-gather.21.cloned.1.call-start = ((), (), s32[]{:S(2)}) async-start(), calls=%async_computation.19 | async-start | bytes 2359296 | tf_op jit(solution)/shard_map/all_gather | solution.py:25
  166.9 4.8 collective-permute-start.1
  180.4 148.3 %all-gather.23.cloned.1.call-start = ((), (), s32[]{:S(2)}) async-start(), calls=%async_computation.20 | async-start | bytes 2359296 | tf_op jit(solution)/shard_map/all_gather | solution.py:25
  281.4 139.3 %reduce-scatter.17.cloned.1.call-start = ((), (), s32[]{:S(2)}) async-start(), calls=%async_computation.12 | async-start | bytes 1310720 | tf_op jit(solution)/shard_map/reduce_scatter | solution.py:278
  387.5 5.6 collective-permute-start.2
  396.4 51.7 %reduce-scatter.15.cloned.1.call-start = ((), (), s32[]{:S(2)}) async-start(), calls=%async_computation.11 | async-start | bytes 1310720 | tf_op jit(solution)/shard_map/reduce_scatter | solution.py:179
  399.2 58.5 %copy-start.26 = (f32[256,512]{1,0:T(8,128)S(1)}, f32[256,512]{1,0:T(8,128)}, u32[]{:S(2)}) copy-start(f32[256,512]{1,0:T(8,128)} %copy-done.25) | copy-start | bytes 1572868
  399.2 58.5 %copy-start.91 = (f32[1,512]{1,0:T(1,128)S(1)}, f32[1,512]{1,0:T(1,128)}, u32[]{:S(2)}) copy-start(f32[1,512]{1,0:T(1,128)} %copy-done.90) | copy-start | bytes 6148
  399.2 58.5 %copy-start.96 = (f32[256]{0:T(256)S(1)}, f32[256]{0:T(256)}, u32[]{:S(2)}) copy-start(f32[256]{0:T(256)} %copy-done.95) | copy-start | bytes 3076
  399.2 122.4 %all-gather.25.cloned.1.call-start = ((), (), s32[]{:S(2)}) async-start(), calls=%async_computation.21 | async-start | bytes 2359296 | tf_op jit(solution)/shard_map/all_gather | solution.py:25
  472.1 147.7 %all-reduce.33.cloned.1.call-start = ((), (), s32[]{:S(2)}) async-start(), calls=%async_computation.16 | async-start | bytes 4194304 | tf_op jit(solution)/shard_map/psum | solution.py:329
  558.5 5.6 collective-permute-start.3
  568.8 117.1 %reduce-scatter.25.cloned.1.call-start = ((), (), s32[]{:S(2)}) async-start(), calls=%async_computation.22 | async-start | bytes 294912
  573.9 182.8 %reduce-scatter.27.cloned.1.call-start = ((), (), s32[]{:S(2)}) async-start(), calls=%async_computation.23 | async-start | bytes 2359296
  586.8 241.5 %reduce-scatter.21.cloned.1.call-start = ((), (), s32[]{:S(2)}) async-start(), calls=%async_computation.14 | async-start | bytes 2359296 | tf_op jit(solution)/shard_map/reduce_scatter | solution.py:313
  590.2 264.4 %reduce-scatter.19.cloned.1.call-start = ((), (), s32[]{:S(2)}) async-start(), calls=%async_computation.13 | async-start | bytes 1310720 | tf_op jit(solution)/shard_map/reduce_scatter | solution.py:278
  595.4 331.6 %reduce-scatter.23.cloned.1.call-start = ((), (), s32[]{:S(2)}) async-start(), calls=%async_computation.15 | async-start | bytes 2359296 | tf_op jit(solution)/shard_map/reduce_scatter | solution.py:316
  598.1 433.8 %all-reduce.35.cloned.1.call-start = ((), (), s32[]{:S(2)}) async-start(), calls=%async_computation.17 | async-start | bytes 4194304 | tf_op jit(solution)/shard_map/psum | solution.py:329
  619.8 234.8 %copy-start.32 = (f32[256,256]{1,0:T(8,128)S(1)}, f32[256,256]{1,0:T(8,128)}, u32[]{:S(2)}) copy-start(f32[256,256]{1,0:T(8,128)} %param.25) | copy-start | bytes 786436
  619.8 234.8 %copy-start.104 = (f32[1,256]{1,0:T(1,128)S(1)}, f32[1,256]{1,0:T(1,128)}, u32[]{:S(2)}) copy-start(f32[1,256]{1,0:T(1,128)} %copy-done.103) | copy-start | bytes 3076
  619.8 234.8 %copy-start.111 = (f32[256]{0:T(256)S(1)}, f32[256]{0:T(256)}, u32[]{:S(2)}) copy-start(f32[256]{0:T(256)} %copy-done.110) | copy-start | bytes 3076
  619.8 246.0 %copy-start.131 = (f32[256]{0:T(256)S(1)}, f32[256]{0:T(256)}, u32[]{:S(2)}) copy-start(f32[256]{0:T(256)} %get-tuple-element.1182) | copy-start | bytes 3076
  619.8 284.5 %copy-start.56 = (f32[256,256]{1,0:T(8,128)S(1)}, f32[256,256]{1,0:T(8,128)}, u32[]{:S(2)}) copy-start(f32[256,256]{1,0:T(8,128)} %get-tuple-element.1267) | copy-start | bytes 786436
  (141 other events, 1175.6 us)
Sparse Core Ops, SparseCore 0:
  9.5 19.4 all-gather.14
  42.5 49.0 all-gather.18
  117.6 23.5 reduce-scatter.12
  143.3 16.6 all-gather.16
  180.5 50.1 all-gather.20
  281.6 47.0 all-gather.22
  396.5 24.1 reduce-scatter.16
  423.2 24.7 reduce-scatter.14
  472.2 49.4 all-gather.24
  568.9 50.8 all-reduce.32
  623.7 62.1 reduce-scatter.24
  689.2 67.4 reduce-scatter.26
  760.8 67.4 reduce-scatter.20
  830.7 23.8 reduce-scatter.18
  857.9 69.0 reduce-scatter.22
  930.5 101.2 all-reduce.34
